TPU v7x, 32 devices: a whole 2x2x4 slice. The times are simulated.
32 devices in a mesh: groups: 2 (over x), section: 16 (over z, y, core).
Axes of the slice: x: 2, y: 2, z: 4, core: 2. Of those that a mesh axis runs over, the one named last changes fastest.
Arguments:
- queries: bfloat16 [4096, 4096], P(('groups', 'section')), parts along dimension 0, may hold values from -400 to 400
- keys: bfloat16 [4096, 256], P(('groups', 'section')), parts along dimension 0, may hold values from -4 to 4
- values: bfloat16 [4096, 256], P(('groups', 'section')), parts along dimension 0, may hold values from -6 to 6
- windows: int32 [32], P('groups'), parts along dimension 0, may hold values from 0 to 1024, as said below
Outputs:
- attended: bfloat16 [4096, 4096], P(('groups', 'section')), parts along dimension 0
- log_total: float32 [4096, 32], P(('groups', 'section')), parts along dimension 0
There are 2 independent parts, one for each index of `groups`. A program takes and returns all parts, laid end to end along the dimension named above; each array names one. Nothing has to cross between parts.
Inputs may be any that keep to these rules, and one draw needn't show every extreme that they name: `windows`: the first slice's window is 0 and the last slice's window is 1024.
All inputs are finite; a program needn't handle non-finite values.
Results may differ from a plain program's by a relative error of at most 0.0055.
Values may be sent and summed in bfloat16 or wider, within the bound.
A program may use at most 64 MiB of HBM per device.

v0:
```python
import functools

import jax
import jax.numpy as jnp
from jax import lax
from jax.experimental import pallas as pl
from jax.experimental.pallas import tpu as pltpu
from jax.sharding import PartitionSpec as P

HD = 128
PLANE = 4
BATCH = 16
SPLIT = 2
PIECES = 2 * SPLIT
ONES = 16
LOG2E = 1.4426950408889634
LN2 = 0.6931471805599453
SCALE2 = HD ** (-0.5) * LOG2E
CONTRACT_LAST = (((1,), (1,)), ((), ()))


def kernel(
    section,
    q_hbm,
    k_hbm,
    v_hbm,
    windows,
    staged,
    log_total,
    q,
    slots,
    kx,
    vt,
    top,
    acc,
    local_sem,
    send_sem,
    recv_sem,
):
    reach = section // 2
    rows = q.shape[0]
    kv_heads = kx.shape[0]
    heads = q.shape[1] // HD
    per_group = heads // kv_heads
    batch = BATCH
    me = lax.axis_index("section")
    z, y, c = me // PLANE, (me // 2) % 2, me % 2
    last_z = section // PLANE - 1

    q_in = pltpu.make_async_copy(q_hbm, q, local_sem.at[0])
    k_in = pltpu.make_async_copy(k_hbm, slots.at[0, 0], local_sem.at[1])
    v_in = pltpu.make_async_copy(v_hbm, slots.at[0, 1], local_sem.at[2])
    k_in.start()
    v_in.start()
    q_in.start()

    barrier = pltpu.get_barrier_semaphore()

    def greet(other):
        pl.semaphore_signal(barrier, inc=1, device_id={"section": other})

    greet(me + 1 - 2 * c)
    greet(me + 2 - 4 * y)
    pl.when(z < last_z)(lambda: greet(me + PLANE))
    pl.when(z > 0)(lambda: greet(me - PLANE))
    pl.semaphore_wait(
        barrier, 2 + (z < last_z).astype(jnp.int32) + (z > 0).astype(jnp.int32)
    )

    def sends(slot):
        found = []
        if slot % PLANE == 0:
            if slot + PLANE <= reach:
                found.append((z < last_z, slot + PLANE, me + PLANE, 0))
            if slot + 2 <= reach:
                found.append((y == 0, slot + 2, me + 2, 1))
            if slot >= 2:
                found.append((y == 1, slot - 2, me - 2, 1))
        if slot + 1 <= reach:
            found.append((c == 0, slot + 1, me + 1, 2))
        if slot >= 1:
            found.append((c == 1, slot - 1, me - 1, 2))
        return found

    def piece_rows(piece):
        size = rows // SPLIT
        return pl.ds(piece % SPLIT * size, size)

    def describe(slot, piece, target, other, kind):
        kind_of, part = piece // SPLIT, piece_rows(piece)
        if slot:
            source = slots.at[slot, kind_of, part]
        else:
            source = (k_hbm, v_hbm)[kind_of].at[part]
        return pltpu.make_async_remote_copy(
            src_ref=source,
            dst_ref=slots.at[target, kind_of, part],
            send_sem=send_sem.at[slot // 2, kind, piece],
            recv_sem=recv_sem.at[target, piece],
            device_id={"section": other},
        )

    def relay(slot, piece):
        for condition, target, other, kind in sends(slot):
            copy = describe(slot, piece, target, other, kind)
            pl.when(condition & (me >= slot))(copy.start)

    def finish(slot, piece):
        for condition, target, other, kind in sends(slot):
            copy = describe(slot, piece, target, other, kind)
            pl.when(condition & (me >= slot))(copy.wait_send)

    def arrive(slot, piece):
        copy = pltpu.make_async_remote_copy(
            src_ref=slots.at[slot, piece // SPLIT, piece_rows(piece)],
            dst_ref=slots.at[slot, piece // SPLIT, piece_rows(piece)],
            send_sem=send_sem.at[0, 0, piece],
            recv_sem=recv_sem.at[slot, piece],
            device_id={"section": me},
        )
        pl.when(me >= slot)(copy.wait_recv)

    window = windows[me]
    takes, groups, rest = [[PLANE]], [[PLANE]], [1, 2, 3]
    for far in range(2 * PLANE, reach + 1, PLANE):
        takes += [[far - PLANE - 2, far] if far == 2 * PLANE else [far], [far - 2]]
        groups += [rest, [far - 1, far]]
        rest = [far - 3, far - 2]
    takes.append([])
    groups.append(rest)
    place = {0: 0}
    for group in groups:
        for slot in group:
            place[slot] = len(place)

    def actual(label):
        if label < PLANE or label % 2 == 0:
            return label
        return label - 2 * c if label % PLANE == 3 else label + 2 * c

    def prepare(label):
        slot = actual(label)
        ages = slot * rows - lax.broadcasted_iota(jnp.int32, (rows, HD), 0)
        seen = (ages <= window) & (me >= slot)
        lane_ages = slot * rows - lax.broadcasted_iota(jnp.int32, (ONES, rows), 1)
        lane_seen = (lane_ages <= window) & (me >= slot)
        span = slice(place[label] * rows, (place[label] + 1) * rows)
        for g in range(kv_heads):
            cols = slice(g * HD, (g + 1) * HD)
            key = slots[slot, 0, :, cols].astype(jnp.float32)
            value = slots[slot, 1, :, cols].astype(jnp.float32)
            if label:
                spare = slots[0, 0, 0:1, cols].astype(jnp.float32)
                key = jnp.where(seen, key, spare)
                value = jnp.where(seen, value, 0.0)
            scaled = key * SCALE2
            high = scaled.astype(jnp.bfloat16)
            low = (scaled - high.astype(jnp.float32)).astype(jnp.bfloat16)
            kx[g, span, 0:HD] = high
            kx[g, span, HD : 2 * HD] = low
            vt[g, 0:HD, span] = value.T.astype(jnp.bfloat16)
            if label:
                counted = jnp.where(lane_seen, 1.0, 0.0)
            else:
                counted = jnp.ones((ONES, rows), jnp.float32)
            vt[g, HD : HD + ONES, span] = counted.astype(jnp.bfloat16)

    def attend(begin, count, first, last):
        span = slice(begin * rows, (begin + count) * rows)
        for number in range(heads // batch):
            g = number * batch // per_group
            columns = [
                slice((number * batch + j) * HD, (number * batch + j + 1) * HD)
                for j in range(batch)
            ]
            stacked = jnp.concatenate([q[:, col] for col in columns], 0)
            doubled = jnp.concatenate([stacked, stacked], 1)
            scores = lax.dot_general(
                kx[g, span, :],
                doubled,
                CONTRACT_LAST,
                preferred_element_type=jnp.float32,
            )
            if first:
                key_pos = lax.broadcasted_iota(jnp.int32, (rows, rows), 0)
                row_pos = lax.broadcasted_iota(jnp.int32, (rows, rows), 1)
                causal = jnp.concatenate([key_pos <= row_pos] * batch, 1)
                scores = jnp.where(causal, scores, -1e30)
            highest = jnp.max(scores, 0, keepdims=True)
            if not first:
                before = top[number]
                highest = jnp.maximum(highest, before)
                factor = jnp.exp2(before - highest)
            weights = jnp.exp2(scores - highest).astype(jnp.bfloat16)
            update = jnp.dot(
                vt[g, :, span], weights, preferred_element_type=jnp.float32
            )
            summed = update[0 : HD + 8]
            if not first:
                summed = summed + acc[number] * factor
            if not last:
                top[number] = highest
                acc[number] = summed
            else:
                total = summed[HD : HD + 1]
                result = summed[0:HD] * (1.0 / total)
                level = highest * LN2 + jnp.log(total)
                for j in range(batch):
                    side = slice(j * rows, (j + 1) * rows)
                    staged[:, columns[j]] = result[:, side].T.astype(jnp.bfloat16)
                    log_total[number * batch + j : number * batch + j + 1, :] = level[
                        :, side
                    ]

    def take(label):
        slot = actual(label)
        for piece in range(PIECES):
            arrive(slot, piece)
            if label % 2 == 0:
                relay(slot, piece)

    def absorb(group, last=False):
        for slot in group:
            if slot % 2:
                take(slot)
            prepare(slot)
        attend(place[group[0]], len(group), False, last)

    for piece in range(PIECES):
        relay(0, piece)
    k_in.wait()
    v_in.wait()
    prepare(0)
    q_in.wait()
    attend(0, 1, True, False)
    for number, group in enumerate(groups):
        for slot in takes[number]:
            take(slot)
        absorb(group, number == len(groups) - 1)
    for slot in range(0, reach + 1, 2):
        for piece in range(PIECES):
            finish(slot, piece)


def solution(mesh):
    section = mesh.shape["section"]
    reach = section // 2

    def on_device(queries, keys, values, windows):
        rows = queries.shape[0]
        heads = queries.shape[1] // HD
        kv_heads = keys.shape[1] // HD
        batches = heads // BATCH
        length = (reach + 1) * rows
        attended, log_total = pl.pallas_call(
            functools.partial(kernel, section),
            out_shape=(
                pltpu.VMEM(queries.shape, jnp.bfloat16),
                pltpu.VMEM((heads, rows), jnp.float32),
            ),
            in_specs=[pl.BlockSpec(memory_space=pl.ANY)] * 3
            + [pl.BlockSpec(memory_space=pltpu.SMEM)],
            out_specs=(
                pl.BlockSpec(memory_space=pltpu.VMEM),
                pl.BlockSpec(memory_space=pltpu.VMEM),
            ),
            scratch_shapes=[
                pltpu.VMEM(queries.shape, jnp.bfloat16),
                pltpu.VMEM((reach + 1, 2) + keys.shape, jnp.bfloat16),
                pltpu.VMEM((kv_heads, length, 2 * HD), jnp.bfloat16),
                pltpu.VMEM((kv_heads, HD + ONES, length), jnp.bfloat16),
                pltpu.VMEM((batches, 1, BATCH * rows), jnp.float32),
                pltpu.VMEM((batches, HD + 8, BATCH * rows), jnp.float32),
                pltpu.SemaphoreType.DMA((3,)),
                pltpu.SemaphoreType.DMA((reach // 2 + 1, 3, PIECES)),
                pltpu.SemaphoreType.DMA((reach + 1, PIECES)),
            ],
            compiler_params=pltpu.CompilerParams(
                collective_id=0, has_side_effects=True
            ),
        )(queries, keys, values, windows)
        return attended, log_total.T

    placed = (
        P(("groups", "section"), None),
        P(("groups", "section"), None),
        P(("groups", "section"), None),
        P("groups"),
    )
    return jax.shard_map(
        on_device,
        mesh=mesh,
        in_specs=placed,
        out_specs=(P(("groups", "section"), None), P(("groups", "section"), None)),
        check_vma=False,
    )
```

profile of v0, /device:TPU:17, one launch (start us, length us, event | category | flops | bytes accessed | tf_op | source)
XLA Modules:
  0.0 21.3 jit_solution(2809966749406518599)
XLA Ops:
  0.6 19.1 %shard_map.59 = (bf16[128,4096]{1,0:T(8,128)(2,1)S(1)}, f32[32,128]{1,0:T(8,128)S(1)}) custom-call(bf16[128,4096]{1,0:T(8,128)(2,1)} %q_hbm.1, bf16[128,256]{1,0:T(8,128)(2,1)} %k_hbm.1, bf16[128,256]{1,0:T(8,128)(2,1)} %v_hbm.1, s32[16]{0:T(128)} %windows.1), custom_call_target="tpu_custom_call" | custom-call | tf_op jit(solution)/shard_map/pallas_call | solution.py:255
  19.7 1.0 %copy.8 = bf16[128,4096]{1,0:T(8,128)(2,1)} copy(bf16[128,4096]{1,0:T(8,128)(2,1)S(1)} %get-tuple-element.6) | data formatting | bytes 2097152
  20.7 0.6 %copy.9 = f32[128,32]{0,1:T(8,128)} copy(f32[128,32]{0,1:T(8,128)S(1)} %bitcast.1) | data formatting | bytes 32768
where the time goes:
time: 21.5 us; the launch traced here: 21.3 us
  Pallas kernels  19.1 us (89%)
  local copies, waits for them, and re-layouts  1.58 us (7%)
  between operations  0.64 us (3%)
    pallas_call x1, Pallas kernels, on_device(): pl.pallas_call(functools.partial(kernel, section), out_shape=(pltpu.VMEM(...  19.1 us
    unnamed x2, local copies, waits for them, and re-layouts  1.58 us

commit v1 on v0

--- a/solution.py
+++ b/solution.py
@@ -13,6 +13,8 @@
 SPLIT = 2
 PIECES = 2 * SPLIT
 ONES = 16
+CHUNK = 4
+CAST_FIRST = True
 LOG2E = 1.4426950408889634
 LN2 = 0.6931471805599453
 SCALE2 = HD ** (-0.5) * LOG2E
@@ -25,14 +27,12 @@
     k_hbm,
     v_hbm,
     windows,
-    staged,
-    log_total,
+    acc,
+    top,
     q,
     slots,
     kx,
     vt,
-    top,
-    acc,
     local_sem,
     send_sem,
     recv_sem,
@@ -198,19 +198,8 @@
             summed = update[0 : HD + 8]
             if not first:
                 summed = summed + acc[number] * factor
-            if not last:
-                top[number] = highest
-                acc[number] = summed
-            else:
-                total = summed[HD : HD + 1]
-                result = summed[0:HD] * (1.0 / total)
-                level = highest * LN2 + jnp.log(total)
-                for j in range(batch):
-                    side = slice(j * rows, (j + 1) * rows)
-                    staged[:, columns[j]] = result[:, side].T.astype(jnp.bfloat16)
-                    log_total[number * batch + j : number * batch + j + 1, :] = level[
-                        :, side
-                    ]
+            top[number] = highest
+            acc[number] = summed
 
     def take(label):
         slot = actual(label)
@@ -242,6 +231,34 @@
             finish(slot, piece)
 
 
+def finish_kernel(acc, top, attended, log_total, staged, level, sems):
+    batches = acc.shape[0]
+    copies = []
+    for number in range(batches):
+        for part in range(BATCH // CHUNK):
+            span = slice(part * CHUNK * HD, (part + 1) * CHUNK * HD)
+            total = acc[number, HD : HD + 1, span]
+            inverse = 1.0 / total
+            levels = top[number, :, span] * LN2 + jnp.log(total)
+            for j in range(CHUNK):
+                head = number * BATCH + part * CHUNK + j
+                side = slice((part * CHUNK + j) * HD, (part * CHUNK + j + 1) * HD)
+                here = slice(j * HD, (j + 1) * HD)
+                result = acc[number, 0:HD, side] * inverse[:, here]
+                staged[:, head * HD : (head + 1) * HD] = result.astype(jnp.bfloat16).T if CAST_FIRST else result.T.astype(jnp.bfloat16)
+                level[head : head + 1, :] = levels[:, here]
+            first = number * BATCH + part * CHUNK
+            cols = pl.ds(first * HD, CHUNK * HD)
+            copy = pltpu.make_async_copy(staged.at[:, cols], attended.at[:, cols], sems.at[len(copies)])
+            copy.start()
+            copies.append(copy)
+    copy = pltpu.make_async_copy(level, log_total, sems.at[len(copies)])
+    copy.start()
+    copies.append(copy)
+    for copy in copies:
+        copy.wait()
+
+
 def solution(mesh):
     section = mesh.shape["section"]
     reach = section // 2
@@ -252,11 +269,11 @@
         kv_heads = keys.shape[1] // HD
         batches = heads // BATCH
         length = (reach + 1) * rows
-        attended, log_total = pl.pallas_call(
+        acc, top = pl.pallas_call(
             functools.partial(kernel, section),
             out_shape=(
-                pltpu.VMEM(queries.shape, jnp.bfloat16),
-                pltpu.VMEM((heads, rows), jnp.float32),
+                pltpu.VMEM((batches, HD + 8, BATCH * rows), jnp.float32),
+                pltpu.VMEM((batches, 1, BATCH * rows), jnp.float32),
             ),
             in_specs=[pl.BlockSpec(memory_space=pl.ANY)] * 3
             + [pl.BlockSpec(memory_space=pltpu.SMEM)],
@@ -269,8 +286,6 @@
                 pltpu.VMEM((reach + 1, 2) + keys.shape, jnp.bfloat16),
                 pltpu.VMEM((kv_heads, length, 2 * HD), jnp.bfloat16),
                 pltpu.VMEM((kv_heads, HD + ONES, length), jnp.bfloat16),
-                pltpu.VMEM((batches, 1, BATCH * rows), jnp.float32),
-                pltpu.VMEM((batches, HD + 8, BATCH * rows), jnp.float32),
                 pltpu.SemaphoreType.DMA((3,)),
                 pltpu.SemaphoreType.DMA((reach // 2 + 1, 3, PIECES)),
                 pltpu.SemaphoreType.DMA((reach + 1, PIECES)),
@@ -279,6 +294,26 @@
                 collective_id=0, has_side_effects=True
             ),
         )(queries, keys, values, windows)
+        acc = pltpu.with_memory_space_constraint(acc, pltpu.VMEM)
+        top = pltpu.with_memory_space_constraint(top, pltpu.VMEM)
+        attended, log_total = pl.pallas_call(
+            finish_kernel,
+            out_shape=(
+                jax.ShapeDtypeStruct(queries.shape, jnp.bfloat16),
+                jax.ShapeDtypeStruct((heads, rows), jnp.float32),
+            ),
+            in_specs=[pl.BlockSpec(memory_space=pltpu.VMEM)] * 2,
+            out_specs=(
+                pl.BlockSpec(memory_space=pl.ANY),
+                pl.BlockSpec(memory_space=pl.ANY),
+            ),
+            scratch_shapes=[
+                pltpu.VMEM(queries.shape, jnp.bfloat16),
+                pltpu.VMEM((heads, rows), jnp.float32),
+                pltpu.SemaphoreType.DMA((heads // CHUNK + 1,)),
+            ],
+            compiler_params=pltpu.CompilerParams(vmem_limit_bytes=16 * 2**20),
+        )(acc, top)
         return attended, log_total.T
 
     placed = (

time: 21.5 us -> 20.9 us (0.972)
  local copies, waits for them, and re-layouts: 1.58 us -> 0 us
  Pallas kernels: 19.1 us -> 20.1 us
    unnamed x2 -> x0, local copies, waits for them, and re-layouts: 1.58 us -> none
    pallas_call x0 -> x1, Pallas kernels: none -> 1.13 us  [on_device(): pl.pallas_call(finish_kernel, out_shape=(jax.ShapeDtypeStruct(queries.sha...]
where the time goes in v1:
time: 20.9 us; the launch traced here: 20.7 us
  Pallas kernels  20.1 us (96%)
  between operations  0.64 us (3%)
    pallas_call x1, Pallas kernels, on_device(): pl.pallas_call(functools.partial(kernel, section), out_shape=(pltpu.VMEM(...  19 us
    pallas_call x1, Pallas kernels, on_device(): pl.pallas_call(finish_kernel, out_shape=(jax.ShapeDtypeStruct(queries.sha...  1.13 us

profile of v1, /device:TPU:17, one launch (start us, length us, event | category | flops | bytes accessed | tf_op | source)
XLA Modules:
  0.0 20.7 jit_solution(15725072417100347244)
XLA Ops:
  0.6 19.0 %shard_map.59 = (f32[2,136,2048]{2,1,0:T(8,128)S(1)}, f32[2,1,2048]{2,1,0:T(1,128)S(1)}) custom-call(bf16[128,4096]{1,0:T(8,128)(2,1)} %q_hbm.1, bf16[128,256]{1,0:T(8,128)(2,1)} %k_hbm.1, bf16[128,256]{1,0:T(8,128)(2,1)} %v_hbm.1, s32[16]{0:T(128)} %windows.1), custom_call_target="tpu_custom_call" | custom-call | tf_op jit(solution)/shard_map/pallas_call | solution.py:272
  19.6 1.1 %shard_map.60 = (bf16[128,4096]{1,0:T(8,128)(2,1)}, f32[32,128]{1,0:T(8,128)}) custom-call(f32[2,136,2048]{2,1,0:T(8,128)S(1)} %get-tuple-element.6.acc, f32[2,1,2048]{2,1,0:T(1,128)S(1)} %get-tuple-element.7.top), custom_call_target="tpu_custom_call" | custom-call | tf_op jit(solution)/shard_map/pallas_call | solution.py:299
